TPU v7x, 32 devices: a whole 2x2x4 slice. The times are simulated.
32 devices in a mesh: segment: 4 (over y, x), seq: 8 (over z, core).
Axes of the slice: x: 2, y: 2, z: 4, core: 2. Of those that a mesh axis runs over, the one named last changes fastest.
Arguments:
- hidden: bfloat16 [4, 8192, 8192], P('segment', 'seq'), may hold values from -6 to 6
- span_lengths: int32 [4, 64], replicated, may hold values from 1 to 512, 8192 in all within a row
- section_of: int32 [4, 64], replicated, may hold values from 0 to 31
- section_live: int32 [32], P('seq'), may hold values 0 or 1
- w_in: bfloat16 [8192, 2048], P('seq'), may hold values from -0.5 to 0.5
- norm_gain: float32 [2048], replicated, may hold values from 0.5 to 1.5
- w_query: bfloat16 [2048, 2048], P(None, 'segment'), may hold values from -0.125 to 0.125
- w_key: bfloat16 [2048, 2048], P(None, 'segment'), may hold values from -0.125 to 0.125
- w_value: bfloat16 [2048, 2048], P(None, 'segment'), may hold values from -0.125 to 0.125
- w_out: bfloat16 [2048, 2048], P('segment'), may hold values from -0.125 to 0.125
Outputs:
- section_out: bfloat16 [32, 2048], P('seq')
All inputs are finite; a program needn't handle non-finite values. No bound on the sum of `section_live` on one device may be relied on, other than what follows from the above.
Results may differ from a plain program's by a relative error of at most 0.007.
Values may be sent and summed in bfloat16 or wider, within the bound.
A program may use at most 128 MiB of HBM per device.

v0:
```python
import jax
import jax.numpy as jnp
from jax import lax
from jax.sharding import PartitionSpec as P

HEAD_DIM = 128


def shards(
    hidden, span_lengths, section_of, section_live, w_in, norm_gain, w_query, w_key, w_value, w_out
):
    tokens = hidden[0]
    seq_count = lax.axis_size("seq")
    seq_index = lax.axis_index("seq")
    segment_index = lax.axis_index("segment")
    tok_count = tokens.shape[0]
    lengths = lax.dynamic_index_in_dim(span_lengths, segment_index, 0, keepdims=False)
    span_ends = jnp.cumsum(lengths)
    span_starts = span_ends - lengths
    positions = seq_index * tok_count + jnp.arange(tok_count, dtype=jnp.int32)
    member = (
        (positions[None, :] >= span_starts[:, None]) & (positions[None, :] < span_ends[:, None])
    ).astype(jnp.bfloat16)
    partial_value = jnp.dot(member, tokens, preferred_element_type=jnp.float32)
    length_float = lengths.astype(jnp.float32)
    sections_here = section_live.shape[0]
    section_total = sections_here * seq_count
    section_ids = jnp.arange(section_total, dtype=jnp.int32)
    own_sections = seq_index * sections_here + jnp.arange(sections_here, dtype=jnp.int32)
    flat_sections = section_of.reshape(-1)
    count_all = jnp.sum(
        (section_ids[:, None] == flat_sections[None, :]).astype(jnp.float32), axis=1
    )
    doc_sections = lax.dynamic_index_in_dim(section_of, segment_index, 0, keepdims=False)
    weighted = partial_value / length_float[:, None]
    doc_onehot = (section_ids[:, None] == doc_sections[None, :]).astype(jnp.float32)
    section_part = jnp.dot(doc_onehot, weighted, precision=lax.Precision.HIGHEST)
    feature_block = lax.psum_scatter(section_part, "seq", scatter_dimension=1, tiled=True)
    doc_total = lax.psum(feature_block, "segment")
    pooled = (doc_total / jnp.maximum(count_all, 1.0)[:, None]).astype(jnp.bfloat16)
    projected = jnp.dot(pooled, w_in, preferred_element_type=jnp.float32)
    section_in = lax.psum_scatter(projected, "seq", scatter_dimension=0, tiled=True)
    scale = lax.rsqrt(jnp.mean(section_in * section_in, axis=1, keepdims=True) + 1e-05)
    normed = (section_in * scale * norm_gain[None, :]).astype(jnp.bfloat16)
    queries = jnp.dot(normed, w_query, preferred_element_type=jnp.float32).astype(jnp.bfloat16)
    keys_here = jnp.dot(normed, w_key, preferred_element_type=jnp.float32).astype(jnp.bfloat16)
    values_here = jnp.dot(normed, w_value, preferred_element_type=jnp.float32).astype(jnp.bfloat16)
    live_here = section_live.astype(jnp.bfloat16)
    keys_all, values_all, live_all = (
        lax.all_gather(keys_here, "seq", axis=0, tiled=True),
        lax.all_gather(values_here, "seq", axis=0, tiled=True),
        lax.all_gather(live_here, "seq", axis=0, tiled=True),
    )
    local_heads = queries.shape[1] // HEAD_DIM
    query_heads = queries.reshape(sections_here, local_heads, HEAD_DIM)
    key_heads = keys_all.reshape(section_total, local_heads, HEAD_DIM)
    value_heads = values_all.reshape(section_total, local_heads, HEAD_DIM)
    scores = jnp.einsum("qhd,khd->hqk", query_heads, key_heads, preferred_element_type=jnp.float32)
    scores = scores / jnp.sqrt(jnp.float32(HEAD_DIM))
    allowed = (live_all[None, :] > 0) | (section_ids[None, :] == own_sections[:, None])
    scores = jnp.where(allowed[None, :, :], scores, jnp.float32(-1e30))
    probs = jax.nn.softmax(scores, axis=-1).astype(jnp.bfloat16)
    attended = jnp.einsum(
        "hqk,khd->qhd", probs, value_heads, preferred_element_type=jnp.float32
    ).astype(jnp.bfloat16)
    attended = attended.reshape(sections_here, local_heads * HEAD_DIM)
    head_terms = jnp.dot(attended, w_out, preferred_element_type=jnp.float32)
    combined = lax.psum(head_terms, "segment")
    return (section_in + combined).astype(jnp.bfloat16)


def solution(mesh):
    in_specs = (
        P("segment", "seq", None),
        P(),
        P(),
        P("seq"),
        P("seq", None),
        P(),
        P(None, "segment"),
        P(None, "segment"),
        P(None, "segment"),
        P("segment", None),
    )
    out_specs = P("seq", None)
    return jax.shard_map(shards, mesh=mesh, in_specs=in_specs, out_specs=out_specs, check_vma=False)
```

profile of v0, /device:TPU:0, one launch (start us, length us, event | category | flops | bytes accessed | tf_op | source)
XLA Modules:
  0.0 217.7 jit_solution(10877947771555918930)
XLA Ops:
  6.5 0.0 copy-start
  6.5 0.0 reduce-scatter.2.cloned.1.call-start
  6.5 0.9 fusion.30
  7.4 0.1 copy.25
  7.5 0.1 reduce-window.7
  7.6 0.1 reduce
  7.7 0.7 bitcast_subtract_fusion
  8.4 8.8 %fusion.3 = f32[64,8192]{1,0:T(8,128)S(1)} fusion(bf16[1,1024,8192]{2,1,0:T(8,128)(2,1)} %param.10, f32[64]{0:T(128)S(1)} %get-tuple-element.6, s32[1024]{0:T(1024)S(1)} %iota_add_fusion, s32[64]{0:T(128)S(1)} %reduce, s32[64]{0:T(128)S(1)} %bitcast_subtract_fusion), kind=kOutput, calls=%fused_computation.3 | convolution fusion | flops 1074462720 | bytes 18879232 | tf_op jit(solution)/shard_map/dot_general | solution.py:24
  17.3 0.0 copy-start.2
  17.3 0.0 copy-start.4
  17.3 0.0 copy-start.3
  17.3 1.8 fusion.25
  19.1 0.0 reduce-scatter.2.cloned.1.call-update
  19.1 0.0 all-reduce.5.cloned.1.call-start
  19.2 0.0 copy-done.2
  19.2 0.1 eq.52
  19.3 0.0 copy-done.4
  19.3 0.0 copy-done.3
  19.3 0.7 fusion.31
  20.6 0.2 dynamic-update-slice
  20.9 18.2 %all-reduce = bf16[32]{0:T(256)(128)(2,1)S(1)} all-reduce(bf16[32]{0:T(256)(128)(2,1)S(1)} %dynamic-update-slice), channel_id=1, replica_groups=mesh['segment'=4,'seq'=8] {'seq'}, use_global_device_ids=true, to_apply=%add | all-reduce | flops 32 | bytes 128
  39.1 0.1 convert_reduce_fusion
  39.2 15.9 %reduce-scatter.2.cloned.1.call-done = f32[32,1024]{1,0:T(8,128)} async-done(((f32[32,8192]{1,0:T(8,128)}), f32[32,1024]{1,0:T(8,128)}) %reduce-scatter.2.cloned.1.call-update) | async-done | bytes 131088 | tf_op jit(solution)/shard_map/reduce_scatter | solution.py:38
  55.1 0.0 all-reduce.5.cloned.1.call-update
  55.1 0.0 all-reduce.7.cloned.1.call-start
  55.8 0.0 copy-start.1
  55.8 42.1 %all-reduce.5.cloned.1.call-done = f32[32,1024]{1,0:T(8,128)} async-done(((f32[32,1024]{1,0:T(8,128)}), f32[32,1024]{1,0:T(8,128)}) %all-reduce.5.cloned.1.call-update) | async-done | bytes 131088 | tf_op jit(solution)/shard_map/psum | solution.py:39
  97.9 3.8 %fusion.20 = f32[32,2048]{1,0:T(8,128)} fusion(bf16[1024,2048]{1,0:T(8,128)(2,1)} %param.14, f32[32,1024]{1,0:T(8,128)} %all-reduce.5.cloned.1.call-done, f32[32]{0:T(128)S(1)} %broadcast_maximum_fusion), kind=kOutput, calls=%fused_computation.24 | convolution fusion | flops 134283264 | bytes 4587648 | tf_op jit(solution)/shard_map/dot_general | solution.py:41
  101.7 0.0 all-reduce.7.cloned.1.call-update
  101.7 0.1 fusion.29
  101.8 55.5 %all-reduce.7.cloned.1.call-done = f32[32,2048]{1,0:T(8,128)} async-done(((f32[32,2048]{1,0:T(8,128)}), f32[32,2048]{1,0:T(8,128)}) %all-reduce.7.cloned.1.call-update) | async-done | bytes 262160
  157.3 1.0 multiply_reduce_fusion
  158.3 0.0 copy-done.1
  158.3 2.0 fusion.11
  160.3 14.1 %all-gather.1 = bf16[8,4,512]{2,1,0:T(4,128)(2,1)S(1)} all-gather(bf16[1,4,512]{2,1,0:T(4,128)(2,1)S(1)} %fusion.11), channel_id=1, replica_groups=mesh['segment'=4,'seq'=8] {'seq'}, dimensions={0}, use_global_device_ids=true | all-gather | bytes 36864 | tf_op jit(solution)/shard_map/all_gather | solution.py:50
  174.4 2.2 fusion.8
  176.6 0.2 fusion.32
  176.8 2.1 fusion.9
  178.8 14.1 %all-gather = bf16[8,4,512]{2,1,0:T(4,128)(2,1)S(1)} all-gather(bf16[1,4,512]{2,1,0:T(4,128)(2,1)S(1)} %fusion.9), channel_id=1, replica_groups=mesh['segment'=4,'seq'=8] {'seq'}, dimensions={0}, use_global_device_ids=true | all-gather | bytes 36864 | tf_op jit(solution)/shard_map/all_gather | solution.py:51
  192.9 0.0 copy-done
  193.0 0.5 fusion.13
  193.5 16.2 %psum.15 = f32[4,2048]{1,0:T(4,128)S(1)} all-reduce(f32[4,2048]{1,0:T(4,128)S(1)} %fusion.13), channel_id=1, replica_groups=mesh['segment'=4,'seq'=8] {'segment'}, use_global_device_ids=true, to_apply=%region_8.9 | all-reduce | flops 8192 | bytes 65536 | tf_op jit(solution)/shard_map/psum | solution.py:68
  209.7 1.5 add_convert_fusion
  (9 shorter events, 0.1 us)
Async XLA Ops:
  6.5 186.4 %copy-start = (bf16[512,2048]{1,0:T(8,128)(2,1)S(1)}, bf16[512,2048]{1,0:T(8,128)(2,1)}, u32[]{:S(2)}) copy-start(bf16[512,2048]{1,0:T(8,128)(2,1)} %param.19) | copy-start | bytes 6291460
  6.5 48.5 %reduce-scatter.2.cloned.1.call-start = ((), (), s32[]{:S(2)}) async-start(), calls=%async_computation.1 | async-start | bytes 1179648 | tf_op jit(solution)/shard_map/reduce_scatter | solution.py:38
  17.3 1.9 copy-start.2
  17.3 2.0 copy-start.4
  17.3 2.0 copy-start.3
  19.1 78.7 %all-reduce.5.cloned.1.call-start = ((), (), s32[]{:S(2)}) async-start(), calls=%async_computation.2 | async-start | bytes 262144 | tf_op jit(solution)/shard_map/psum | solution.py:39
  55.1 102.2 %all-reduce.7.cloned.1.call-start = ((), (), s32[]{:S(2)}) async-start(), calls=%async_computation.3 | async-start | bytes 524288
  55.8 102.5 %copy-start.1 = (f32[2048]{0:T(1024)S(1)}, f32[2048]{0:T(1024)}, u32[]{:S(2)}) copy-start(f32[2048]{0:T(1024)} %param.15) | copy-start | bytes 24580
Sparse Core Ops, SparseCore 0:
  19.3 35.7 reduce-scatter.1
  58.0 39.8 all-reduce.4
  101.9 55.4 all-reduce.6
where the time goes:
time: 218 us
  waiting for transfers between devices  113 us (52%)
  blocking collectives  62.6 us (29%)
  matrix products  21.3 us (10%)
  between operations  14.5 us (7%)
  other arithmetic  4.58 us (2%)
    unnamed x4, waiting for transfers between devices  55.5 us
    psum x1, waiting for transfers between devices, shards(): doc_total = lax.psum(feature_block, 'segment')  42.1 us
    unnamed x1, blocking collectives  18.2 us
    psum x1, blocking collectives, shards(): combined = lax.psum(head_terms, 'segment')  16.2 us
    reduce_scatter x1, waiting for transfers between devices, shards(): lax.psum_scatter(section_part, 'seq', scatter_dimension=1, tiled=True)  15.9 us
    all_gather x1, blocking collectives, shards(): lax.all_gather(keys_here, 'seq', axis=0, tiled=True)  14.1 us
    all_gather x1, blocking collectives, shards(): lax.all_gather(values_here, 'seq', axis=0, tiled=True)  14.1 us
    dot_general x1, matrix products, shards(): partial_value = jnp.dot(member, tokens, preferred_element_type=jnp.float32)  8.85 us
  transfers between devices with their start and end apart: 3, of which 3 were waited for; matrix products, arithmetic and copies ran while one was open for 1% of the time, Pallas kernels for 0%

commit v1 on v0

--- a/solution.py
+++ b/solution.py
@@ -36,7 +36,11 @@
     doc_onehot = (section_ids[:, None] == doc_sections[None, :]).astype(jnp.float32)
     section_part = jnp.dot(doc_onehot, weighted, precision=lax.Precision.HIGHEST)
     feature_block = lax.psum_scatter(section_part, "seq", scatter_dimension=1, tiled=True)
-    doc_total = lax.psum(feature_block, "segment")
+    doc_total = feature_block
+    for hop in (1, 2):
+        doc_total = doc_total + lax.ppermute(
+            doc_total, "segment", [(dev, dev ^ hop) for dev in range(4)]
+        )
     pooled = (doc_total / jnp.maximum(count_all, 1.0)[:, None]).astype(jnp.bfloat16)
     projected = jnp.dot(pooled, w_in, preferred_element_type=jnp.float32)
     section_in = lax.psum_scatter(projected, "seq", scatter_dimension=0, tiled=True)

time: 218 us -> 185 us (0.85)
  waiting for transfers between devices: 113 us -> 77.3 us
    psum x1 -> x0, waiting for transfers between devices: 42.1 us -> none  [shards(): doc_total = lax.psum(feature_block, 'segment')]
    ppermute x0 -> x2, waiting for transfers between devices: none -> 7.42 us  [shards(): lax.ppermute(doc_total, 'segment', [(dev, dev ^ hop) for dev in range(4)])]
    unnamed x4 -> x3, waiting for transfers between devices: 55.5 us -> 54 us
  transfers between devices with their start and end apart: 3 -> 4, of which waited for: 3 -> 4; matrix products, arithmetic and copies ran while one was open for 1% -> 1% of each run, Pallas kernels for 0% -> 0%
where the time goes in v1:
time: 185 us
  waiting for transfers between devices  77.3 us (42%)
  blocking collectives  62.6 us (34%)
  matrix products  21.3 us (12%)
  between operations  14.8 us (8%)
  other arithmetic  5.5 us (3%)
  starting transfers between devices  2.18 us (1%)
    unnamed x3, waiting for transfers between devices  54 us
    unnamed x1, blocking collectives  18.2 us
    psum x1, blocking collectives, shards(): combined = lax.psum(head_terms, 'segment')  16.2 us
    reduce_scatter x1, waiting for transfers between devices, shards(): lax.psum_scatter(section_part, 'seq', scatter_dimension=1, tiled=True)  15.9 us
    all_gather x1, blocking collectives, shards(): lax.all_gather(keys_here, 'seq', axis=0, tiled=True)  14.1 us
    all_gather x1, blocking collectives, shards(): lax.all_gather(values_here, 'seq', axis=0, tiled=True)  14.1 us
    dot_general x1, matrix products, shards(): partial_value = jnp.dot(member, tokens, preferred_element_type=jnp.float32)  8.85 us
    ppermute x2, waiting for transfers between devices, shards(): lax.ppermute(doc_total, 'segment', [(dev, dev ^ hop) for dev in range(4)])  7.42 us
  transfers between devices with their start and end apart: 4, of which 4 were waited for; matrix products, arithmetic and copies ran while one was open for 1% of the time, Pallas kernels for 0%

profile of v1, /device:TPU:0, one launch (start us, length us, event | category | flops | bytes accessed | tf_op | source)
XLA Modules:
  0.0 184.8 jit_solution(5131011088343930283)
XLA Ops:
  6.5 0.0 copy-start
  6.5 0.0 reduce-scatter.2.cloned.1.call-start
  6.5 0.9 fusion.30
  7.4 0.1 copy.25
  7.5 0.1 reduce-window.7
  7.6 0.1 reduce
  7.7 0.7 bitcast_subtract_fusion
  8.4 8.8 %fusion.3 = f32[64,8192]{1,0:T(8,128)S(1)} fusion(bf16[1,1024,8192]{2,1,0:T(8,128)(2,1)} %param.10, f32[64]{0:T(128)S(1)} %get-tuple-element.6, s32[1024]{0:T(1024)S(1)} %iota_add_fusion, s32[64]{0:T(128)S(1)} %reduce, s32[64]{0:T(128)S(1)} %bitcast_subtract_fusion), kind=kOutput, calls=%fused_computation.3 | convolution fusion | flops 1074462720 | bytes 18879232 | tf_op jit(solution)/shard_map/dot_general | solution.py:24
  17.3 0.0 copy-start.2
  17.3 0.0 copy-start.4
  17.3 0.0 copy-start.3
  17.3 1.8 fusion.25
  19.1 0.0 reduce-scatter.2.cloned.1.call-update
  19.1 0.0 all-reduce.4.cloned.1.call-start
  19.2 0.0 copy-done.2
  19.2 0.1 eq.52
  19.3 0.0 copy-done.4
  19.3 0.0 copy-done.3
  19.3 0.7 fusion.31
  20.6 0.2 dynamic-update-slice
  20.9 18.2 %all-reduce = bf16[32]{0:T(256)(128)(2,1)S(1)} all-reduce(bf16[32]{0:T(256)(128)(2,1)S(1)} %dynamic-update-slice), channel_id=1, replica_groups=mesh['segment'=4,'seq'=8] {'seq'}, use_global_device_ids=true, to_apply=%add | all-reduce | flops 32 | bytes 128
  39.1 0.1 convert_reduce_fusion
  39.2 15.9 %reduce-scatter.2.cloned.1.call-done = f32[32,1024]{1,0:T(8,128)} async-done(((f32[32,8192]{1,0:T(8,128)}), f32[32,1024]{1,0:T(8,128)}) %reduce-scatter.2.cloned.1.call-update) | async-done | bytes 131088 | tf_op jit(solution)/shard_map/reduce_scatter | solution.py:38
  55.1 1.0 collective-permute-start
  56.1 4.1 %collective-permute-done = f32[32,1024]{1,0:T(8,128)S(1)} collective-permute-done((f32[32,1024]{1,0:T(8,128)}, f32[32,1024]{1,0:T(8,128)S(1)}, u32[]{:S(2)}, u32[]{:S(2)}) %collective-permute-start) | collective-permute-done | bytes 131104 | tf_op jit(solution)/shard_map/ppermute | solution.py:41
  60.3 0.9 add.51
  61.2 1.1 collective-permute-start.1
  62.9 0.0 copy-start.1
  62.9 3.3 %collective-permute-done.1 = f32[32,1024]{1,0:T(8,128)S(1)} collective-permute-done((f32[32,1024]{1,0:T(8,128)S(1)}, f32[32,1024]{1,0:T(8,128)S(1)}, u32[]{:S(2)}, u32[]{:S(2)}) %collective-permute-start.1) | collective-permute-done | bytes 131104 | tf_op jit(solution)/shard_map/ppermute | solution.py:41
  66.2 3.8 %fusion.20 = f32[32,2048]{1,0:T(8,128)} fusion(bf16[1024,2048]{1,0:T(8,128)(2,1)} %param.14, f32[32,1024]{1,0:T(8,128)S(1)} %add.51, f32[32,1024]{1,0:T(8,128)S(1)} %collective-permute-done.1, f32[32]{0:T(128)S(1)} %broadcast_maximum_fusion), kind=kOutput, calls=%fused_computation.24 | convolution fusion | flops 134316032 | bytes 4718720 | tf_op jit(solution)/shard_map/dot_general | solution.py:45
  70.0 0.0 all-reduce.4.cloned.1.call-update
  70.0 0.1 fusion.29
  70.1 54.0 %all-reduce.4.cloned.1.call-done = f32[32,2048]{1,0:T(8,128)} async-done(((f32[32,2048]{1,0:T(8,128)}), f32[32,2048]{1,0:T(8,128)}) %all-reduce.4.cloned.1.call-update) | async-done | bytes 262160
  124.1 1.0 multiply_reduce_fusion
  125.0 0.0 copy-done.1
  125.1 2.0 %fusion.11 = bf16[1,4,512]{2,1,0:T(4,128)(2,1)S(1)} fusion(bf16[2048,512]{1,0:T(8,128)(2,1)} %param.17, f32[32,2048]{1,0:T(8,128)} %all-reduce.4.cloned.1.call-done, u32[]{:T(128)S(6)} %multiply.11, f32[2048]{0:T(1024)S(1)} %copy-done.1, f32[4]{0:T(128)S(1)} %add_rsqrt_fusion), kind=kOutput, calls=%fused_computation.14 | convolution fusion | flops 8415232 | bytes 2142228 | tf_op jit(solution)/shard_map/dot_general | solution.py:50
  127.1 14.1 %all-gather.1 = bf16[8,4,512]{2,1,0:T(4,128)(2,1)S(1)} all-gather(bf16[1,4,512]{2,1,0:T(4,128)(2,1)S(1)} %fusion.11), channel_id=1, replica_groups=mesh['segment'=4,'seq'=8] {'seq'}, dimensions={0}, use_global_device_ids=true | all-gather | bytes 36864 | tf_op jit(solution)/shard_map/all_gather | solution.py:54
  141.2 2.2 %fusion.8 = f32[4,4,32]{2,1,0:T(4,128)S(1)} fusion(bf16[2048,512]{1,0:T(8,128)(2,1)} %param.16, bf16[32,4,128]{2,1,0:T(4,128)(2,1)S(1)} %reshape.108, pred[4,32]{1,0:T(4,128)(4,1)S(1)} %fusion.29, f32[32,2048]{1,0:T(8,128)} %all-reduce.4.cloned.1.call-done, u32[]{:T(128)S(6)} %multiply.11, f32[2048]{0:T(1024)S(1)} %copy-done.1, f32[4]{0:T(128)S(1)} %add_rsqrt_fusion), kind=kOutput, calls=%fused_computation.7 | convolution fusion | flops 8547328 | bytes 2173076 | tf_op jit(solution)/shard_map/qhd,khd->hqk/dot_general | solution.py:62
  143.4 0.2 fusion.32
  143.5 2.1 %fusion.9 = bf16[1,4,512]{2,1,0:T(4,128)(2,1)S(1)} fusion(bf16[2048,512]{1,0:T(8,128)(2,1)} %param.18, f32[32,2048]{1,0:T(8,128)} %all-reduce.4.cloned.1.call-done, u32[]{:T(128)S(6)} %multiply.11, f32[2048]{0:T(1024)S(1)} %copy-done.1, f32[4]{0:T(128)S(1)} %add_rsqrt_fusion), kind=kOutput, calls=%fused_computation.12 | convolution fusion | flops 8415232 | bytes 2142228 | tf_op jit(solution)/shard_map/dot_general | solution.py:51
  145.6 14.1 %all-gather = bf16[8,4,512]{2,1,0:T(4,128)(2,1)S(1)} all-gather(bf16[1,4,512]{2,1,0:T(4,128)(2,1)S(1)} %fusion.9), channel_id=1, replica_groups=mesh['segment'=4,'seq'=8] {'seq'}, dimensions={0}, use_global_device_ids=true | all-gather | bytes 36864 | tf_op jit(solution)/shard_map/all_gather | solution.py:55
  159.7 0.0 copy-done
  159.7 0.5 fusion.13
  160.3 16.2 %psum.7 = f32[4,2048]{1,0:T(4,128)S(1)} all-reduce(f32[4,2048]{1,0:T(4,128)S(1)} %fusion.13), channel_id=1, replica_groups=mesh['segment'=4,'seq'=8] {'segment'}, use_global_device_ids=true, to_apply=%region_7.8 | all-reduce | flops 8192 | bytes 65536 | tf_op jit(solution)/shard_map/psum | solution.py:72
  176.5 1.5 add_convert_fusion
  (9 shorter events, 0.1 us)
Async XLA Ops:
  6.5 153.2 %copy-start = (bf16[512,2048]{1,0:T(8,128)(2,1)S(1)}, bf16[512,2048]{1,0:T(8,128)(2,1)}, u32[]{:S(2)}) copy-start(bf16[512,2048]{1,0:T(8,128)(2,1)} %param.19) | copy-start | bytes 6291460
  6.5 48.5 %reduce-scatter.2.cloned.1.call-start = ((), (), s32[]{:S(2)}) async-start(), calls=%async_computation.1 | async-start | bytes 1179648 | tf_op jit(solution)/shard_map/reduce_scatter | solution.py:38
  17.3 1.9 %copy-start.2 = (s32[4,64]{1,0:T(4,128)S(1)}, s32[4,64]{1,0:T(4,128)}, u32[]{:S(2)}) copy-start(s32[4,64]{1,0:T(4,128)} %param.12) | copy-start | bytes 3076
  17.3 2.0 %copy-start.4 = (s32[4]{0:T(128)S(1)}, s32[4]{0:T(128)}, u32[]{:S(2)}) copy-start(s32[4]{0:T(128)} %param.13) | copy-start | bytes 52
  17.3 2.0 %copy-start.3 = (u32[32]{0:T(128)S(1)}, u32[32]{0:T(128)}, u32[]{:S(2)}) copy-start(u32[32]{0:T(128)} %constant.45) | copy-start | bytes 388
  19.1 104.9 %all-reduce.4.cloned.1.call-start = ((), (), s32[]{:S(2)}) async-start(), calls=%async_computation.2 | async-start | bytes 524288
  55.1 5.2 %collective-permute-start = (f32[32,1024]{1,0:T(8,128)}, f32[32,1024]{1,0:T(8,128)S(1)}, u32[]{:S(2)}, u32[]{:S(2)}) collective-permute-start(f32[32,1024]{1,0:T(8,128)} %reduce-scatter.2.cloned.1.call-done), channel_id=1, source_target_pairs={{0,8},{8,0},{16,24},{24,16},{1,9},{9,1},{17,25},{25,17},{2,10},{10... | collective-permute-start | bytes 393224 | tf_op jit(solution)/shard_map/ppermute | solution.py:41
  61.2 5.0 %collective-permute-start.1 = (f32[32,1024]{1,0:T(8,128)S(1)}, f32[32,1024]{1,0:T(8,128)S(1)}, u32[]{:S(2)}, u32[]{:S(2)}) collective-permute-start(f32[32,1024]{1,0:T(8,128)S(1)} %add.51), channel_id=1, source_target_pairs={{0,16},{8,24},{16,0},{24,8},{1,17},{9,25},{17,1},{25,9},{2,18},{10... | collective-permute-start | bytes 393224 | tf_op jit(solution)/shard_map/ppermute | solution.py:41
  62.9 62.1 %copy-start.1 = (f32[2048]{0:T(1024)S(1)}, f32[2048]{0:T(1024)}, u32[]{:S(2)}) copy-start(f32[2048]{0:T(1024)} %param.15) | copy-start | bytes 24580
Sparse Core Ops, SparseCore 0:
  19.3 35.7 reduce-scatter.1
  70.1 53.8 all-reduce.3
